TPU v7x, 32 devices: a whole 2x2x4 slice. The times are simulated.
32 devices in a mesh: cell: 8 (over z, x), tile: 4 (over y, core).
Axes of the slice: x: 2, y: 2, z: 4, core: 2. Of those that a mesh axis runs over, the one named last changes fastest.
Arguments:
- gaussians: float32 [59, 32768], P(None, 'cell'), as said below
- tile_lists: int32 [8, 32, 256], P('cell', 'tile'), may hold values from 0 to 4095, as said below
- list_blocks: int32 [8, 32], P('cell', 'tile'), may hold values from 1 to 2, as said below
- cell_order: int32 [8], replicated, may hold values from 0 to 7, each once
- view_vector: float32 [3], replicated, may hold values from 0.5 to 1
- cotangent: float32 [3, 32, 256], P(None, 'tile'), may hold values from -6 to 6
Outputs:
- rendered: float32 [3, 32, 256], P(None, 'tile')
- gaussian_grads: float32 [59, 32768], P(None, ('cell', 'tile'))
Inputs may be any that keep to these rules, and one draw needn't show every extreme that they name: `gaussians`: Rows: 0-1 center in pixels, 2 depth between 4 and 8, 3-5 log scales, 6-9 a quaternion whose first entry lies between 1 and 2, 10 opacity logit, 11-58 colour coefficients, 16 for each channel in turn. `tile_lists`: indices are local to the cell's block of 4096 Gaussians. Only the first 128 * list_blocks[c,k] entries of the list of cell c and tile k are used; every cell has tiles with the most and the least.
All inputs are finite; a program needn't handle non-finite values.
Results may differ from a plain program's by a relative error of at most 0.0003.
Values sent between devices are 32-bit elements; how exact they have to be, the bound alone decides.
A program may use at most 64 MiB of HBM per device.

v0:
```python
import functools

import jax
import jax.numpy as jnp
from jax import lax
from jax.experimental import pallas as pl
from jax.experimental.pallas import tpu as pltpu
from jax.sharding import PartitionSpec as P

TILE_SIDE = 16
LANES = 128
CHUNKS = 4
UNROLL = 4
ROWS = 16
BACKGROUND = 1.0
FOCAL = 6.0
BLUR = 0.3
F32 = jnp.float32
MESH = pl.DeviceIdType.MESH


def harmonic_basis(vx, vy, vz):
    norm = jnp.sqrt(vx * vx + vy * vy + vz * vz)
    x, y, z = vx / norm, vy / norm, vz / norm
    return [
        0.28209479177387814 + 0.0 * x,
        -0.4886025119029199 * y,
        0.4886025119029199 * z,
        -0.4886025119029199 * x,
        1.0925484305920792 * x * y,
        -1.0925484305920792 * y * z,
        0.31539156525252005 * (2.0 * z * z - x * x - y * y),
        -1.0925484305920792 * x * z,
        0.5462742152960396 * (x * x - y * y),
        -0.5900435899266435 * y * (3.0 * x * x - y * y),
        2.890611442640554 * x * y * z,
        -0.4570457994644658 * y * (4.0 * z * z - x * x - y * y),
        0.3731763325901154 * z * (2.0 * z * z - 3.0 * x * x - 3.0 * y * y),
        -0.4570457994644658 * x * (4.0 * z * z - x * x - y * y),
        1.445305721320277 * z * (x * x - y * y),
        -0.5900435899266435 * x * (x * x - 3.0 * y * y),
    ]


def conic(depth, s0, s1, s2, q0, q1, q2, q3):
    scales = [jnp.exp(2.0 * s) for s in (s0, s1, s2)]
    norm = jnp.sqrt(q0 * q0 + q1 * q1 + q2 * q2 + q3 * q3)
    w, a, b, c = q0 / norm, q1 / norm, q2 / norm, q3 / norm
    row_one = (1.0 - 2.0 * (b * b + c * c), 2.0 * (a * b - w * c), 2.0 * (a * c + w * b))
    row_two = (2.0 * (a * b + w * c), 1.0 - 2.0 * (a * a + c * c), 2.0 * (b * c - w * a))
    ratio = FOCAL / depth
    zoom = ratio * ratio
    xx = zoom * sum(row_one[k] * row_one[k] * scales[k] for k in range(3)) + BLUR
    xy = zoom * sum(row_one[k] * row_two[k] * scales[k] for k in range(3))
    yy = zoom * sum(row_two[k] * row_two[k] * scales[k] for k in range(3)) + BLUR
    det = xx * yy - xy * xy
    return yy / det, -xy / det, xx / det


def sigmoid(x):
    return 1.0 / (1.0 + jnp.exp(-x))


def pick(values, lane):
    return jnp.take_along_axis(values, lane, axis=1, mode="promise_in_bounds")


def harmonic_rows(view_ref, first, rows):
    shape = (rows, LANES)
    vx, vy, vz = (jnp.full(shape, view_ref[k], F32) for k in range(3))
    row = lax.broadcasted_iota(jnp.int32, shape, 0)
    out = jnp.zeros(shape, F32)
    for k, value in enumerate(harmonic_basis(vx, vy, vz)):
        out = jnp.where(row == first + k, value, out)
    return out


def project_all(gauss_ref, view_ref, rows_ref, table_ref, loads):
    blocks = gauss_ref.shape[1] // LANES
    weights = harmonic_rows(view_ref, 3, 24)
    for k in range(blocks):
        if k % (blocks // CHUNKS) == 0:
            loads[k // (blocks // CHUNKS)].wait()
        cols = pl.ds(k * LANES, LANES)
        for r in range(11):
            rows_ref[r, pl.ds(k, 1), :] = gauss_ref[pl.ds(r, 1), cols]
        for ch in range(3):
            start = 8 + 16 * ch
            size = min(24, gauss_ref.shape[0] - start)
            part = gauss_ref[pl.ds(start, size), cols] * weights[:size]
            table_ref[6 + ch, pl.ds(k, 1), :] = 0.5 + jnp.sum(part, axis=0, keepdims=True)
    a, b, c = conic(*[rows_ref[r] for r in range(2, 10)])
    table_ref[0] = rows_ref[0]
    table_ref[1] = rows_ref[1]
    table_ref[2] = a
    table_ref[3] = b
    table_ref[4] = c
    table_ref[5] = sigmoid(rows_ref[10])


def gather_all(lists_ref, blocks_ref, table_ref, picked_ref):
    tiles, length = lists_ref.shape[1], lists_ref.shape[2]
    shape = (tiles, LANES)
    row = lax.broadcasted_iota(jnp.int32, shape, 0)
    lane = lax.broadcasted_iota(jnp.int32, shape, 1)
    limit = jnp.zeros(shape, jnp.int32)
    for t in range(tiles):
        limit = jnp.where(row == t, blocks_ref[0, t] * LANES, limit)
    row_of_tile = lax.axis_index("tile")
    centre_x = (row * TILE_SIDE + TILE_SIDE // 2).astype(F32)
    centre_y = jnp.full(shape, row_of_tile * TILE_SIDE + TILE_SIDE // 2, jnp.int32).astype(F32)
    for part in range(length // LANES):
        cols = pl.ds(part * LANES, LANES)
        index = lists_ref[0, :, cols]
        high = index // LANES
        low = index - high * LANES
        values = [jnp.zeros(shape, F32) for _ in range(9)]
        for k in range(table_ref.shape[1]):
            hit = high == k
            for r in range(9):
                line = jnp.broadcast_to(table_ref[r, pl.ds(k, 1), :], shape)
                values[r] = jnp.where(hit, pick(line, low), values[r])
        values[0] = values[0] - centre_x
        values[1] = values[1] - centre_y
        values[5] = jnp.where(lane + part * LANES < limit, values[5], 0.0)
        for r in range(9):
            picked_ref[r, :, cols] = values[r]


def split(value):
    top = value.astype(jnp.bfloat16)
    return top, (value - top.astype(F32)).astype(jnp.bfloat16)


def dot(a, b):
    return jnp.dot(a, b, preferred_element_type=F32)


def dot_rows(a, b):
    return lax.dot_general(a, b, (((1,), (1,)), ((), ())), preferred_element_type=F32)


def dot_columns(a, b):
    return lax.dot_general(a, b, (((0,), (0,)), ((), ())), preferred_element_type=F32)


def stacked(rows):
    shape = (ROWS, rows[0].shape[1])
    line = lax.broadcasted_iota(jnp.int32, shape, 0)
    out = jnp.zeros(shape, F32)
    for n, row in enumerate(rows):
        out = jnp.where(line == n, row.astype(F32), out)
    return out.astype(jnp.bfloat16)


def halves(rows):
    pieces = [split(row) for row in rows]
    return [p[0] for p in pieces], [p[1] for p in pieces]


def triangles(tri_ref):
    shape = tri_ref.shape[1:]
    row = lax.broadcasted_iota(jnp.int32, shape, 0)
    col = lax.broadcasted_iota(jnp.int32, shape, 1)
    tri_ref[0] = jnp.where(row < col, 1.0, 0.0).astype(jnp.bfloat16)
    tri_ref[1] = jnp.where(row > col, 1.0, 0.0).astype(jnp.bfloat16)


def moment_basis(pixels):
    pixel = lax.broadcasted_iota(jnp.int32, (1, pixels), 1)
    half = 0.5 * (TILE_SIDE - 1)
    px = (pixel % TILE_SIDE).astype(F32) - half
    py = (pixel // TILE_SIDE).astype(F32) - half
    return stacked([jnp.ones_like(px), px, py, px * px, px * py, py * py])


def forward(me, picked_ref, tri_ref, ratio_ref, weight_ref, parts_ref, logs_ref, seen_ref):
    tiles, length = picked_ref.shape[1], picked_ref.shape[2]
    lines = weight_ref.shape[1] // TILE_SIDE
    half = 0.5 * (TILE_SIDE - 1)

    def one_tile(t, _):
        cx, cy, a, b, c, op, c0, c1, c2 = (picked_ref[r, pl.ds(t, 1), :] for r in range(9))
        dx = lax.broadcasted_iota(jnp.int32, (TILE_SIDE, length), 0).astype(F32) - half - cx
        square = (-0.5 * a) * dx * dx
        cross = -b * dx
        curve = -0.5 * c
        for y in range(lines):
            rows = pl.ds(y * TILE_SIDE, TILE_SIDE)
            dy = (y - half) - cy
            alpha = op * jnp.exp(square + cross * dy + curve * dy * dy)
            keep = 1.0 - alpha
            top, rest = split(jnp.log(keep))
            logs_ref[0, rows, :] = top
            logs_ref[1, rows, :] = rest
            weight_ref[t, rows, :] = alpha
            ratio_ref[t, rows, :] = alpha / keep
        upper = tri_ref[0]
        before = dot(logs_ref[0], upper) + dot(logs_ref[1], upper)
        for y in range(lines):
            rows = pl.ds(y * TILE_SIDE, TILE_SIDE)
            weight = weight_ref[t, rows, :] * jnp.exp(before[y * TILE_SIDE : (y + 1) * TILE_SIDE])
            weight_ref[t, rows, :] = weight
            top, rest = split(weight)
            parts_ref[t, 0, rows, :] = top
            parts_ref[t, 1, rows, :] = rest
        tops, rests = halves([c0, c1, c2])
        tint = stacked(tops + rests)
        colour = dot_rows(tint, parts_ref[t, 0]) + dot_rows(tint, parts_ref[t, 1])
        for ch in range(3):
            seen_ref[me, ch, pl.ds(t, 1), :] = colour[ch : ch + 1] + colour[3 + ch : 4 + ch]
        ones = jnp.ones((ROWS, length), jnp.bfloat16)
        total = dot_rows(ones, logs_ref[0]) + dot_rows(ones, logs_ref[1])
        seen_ref[me, 3, pl.ds(t, 1), :] = jnp.exp(total[:1])
        return 0

    lax.fori_loop(0, tiles, one_tile, 0, unroll=UNROLL)


def backward(picked_ref, tri_ref, ratio_ref, weight_ref, parts_ref, logs_ref, tint_ref, grads_ref):
    tiles, length = picked_ref.shape[1], picked_ref.shape[2]
    lines = weight_ref.shape[1] // TILE_SIDE
    basis = moment_basis(weight_ref.shape[1])

    def one_tile(t, _):
        cx, cy = (picked_ref[r, pl.ds(t, 1), :] for r in range(2))
        tops, rests = halves([picked_ref[6 + ch, pl.ds(t, 1), :] for ch in range(3)])
        glow, faint = halves([tint_ref[ch, pl.ds(t, 1), :] for ch in range(4)])
        light = dot_columns(stacked(glow[:3] + glow[:3] + faint[:3]), stacked(tops + rests + tops))
        ones = jnp.ones((ROWS, length), jnp.bfloat16)
        for y in range(lines):
            rows = pl.ds(y * TILE_SIDE, TILE_SIDE)
            lit = weight_ref[t, rows, :] * light[y * TILE_SIDE : (y + 1) * TILE_SIDE]
            weight_ref[t, rows, :] = lit
            top, rest = split(lit)
            logs_ref[0, rows, :] = top
            logs_ref[1, rows, :] = rest
        lower = tri_ref[1]
        later = dot(logs_ref[0], lower) + dot(logs_ref[1], lower)
        later = later + dot_columns(stacked([glow[3], faint[3]]), ones)
        for y in range(lines):
            rows = pl.ds(y * TILE_SIDE, TILE_SIDE)
            slope = weight_ref[t, rows, :] - ratio_ref[t, rows, :] * later[y * TILE_SIDE : (y + 1) * TILE_SIDE]
            top, rest = split(slope)
            logs_ref[2, rows, :] = top
            logs_ref[3, rows, :] = rest
        sums = dot(basis, logs_ref[2]) + dot(basis, logs_ref[3])
        m0, mx, my, mxx, mxy, myy = (sums[n : n + 1] for n in range(6))
        here = pl.ds(t, 1)
        grads_ref[0, here, :] = mx - cx * m0
        grads_ref[1, here, :] = my - cy * m0
        grads_ref[2, here, :] = mxx - 2.0 * cx * mx + cx * cx * m0
        grads_ref[3, here, :] = mxy - cx * my - cy * mx + cx * cy * m0
        grads_ref[4, here, :] = myy - 2.0 * cy * my + cy * cy * m0
        grads_ref[5, here, :] = m0
        tint = stacked(glow[:3] + faint[:3])
        colour = dot(tint, parts_ref[t, 0]) + dot(tint, parts_ref[t, 1])
        for ch in range(3):
            grads_ref[6 + ch, here, :] = colour[ch : ch + 1] + colour[3 + ch : 4 + ch]
        return 0

    lax.fori_loop(0, tiles, one_tile, 0, unroll=UNROLL)


def scatter_all(lists_ref, grads_ref, spread_ref, hot_ref, share_ref, blocks):
    tiles, length = grads_ref.shape[1], grads_ref.shape[2]
    for t in range(tiles):
        index = lists_ref[0, pl.ds(t, 1), :]
        high = index // LANES
        low = index - high * LANES
        cols = pl.ds(t * length, length)
        line = lax.broadcasted_iota(jnp.int32, (LANES, length), 0)
        hot_ref[:, cols] = jnp.where(line == low, 1.0, 0.0).astype(jnp.bfloat16)
        hit = lax.broadcasted_iota(jnp.int32, (blocks, length), 0) == high
        for r in range(9):
            value = grads_ref[r, pl.ds(t, 1), :]
            top = value.astype(jnp.bfloat16).astype(F32)
            rest = value - top
            rows = pl.ds(r * blocks, blocks)
            spread_ref[0, rows, cols] = jnp.where(hit, top, 0.0).astype(jnp.bfloat16)
            spread_ref[1, rows, cols] = jnp.where(hit, rest, 0.0).astype(jnp.bfloat16)
    dims = (((1,), (1,)), ((), ()))
    hot = hot_ref[...]
    total = lax.dot_general(spread_ref[0], hot, dims, preferred_element_type=F32)
    total = total + lax.dot_general(spread_ref[1], hot, dims, preferred_element_type=F32)
    shares, _, lines, _ = share_ref.shape
    for s in range(shares):
        for r in range(9):
            share_ref[s, r] = total[r * blocks + s * lines : r * blocks + (s + 1) * lines]


def pull_back(gauss_ref, view_ref, own_ref, grads, out_ref):
    lines = own_ref.shape[1]
    base = lax.axis_index("tile") * (lines * LANES)
    for k in range(lines):
        cols = pl.ds(pl.multiple_of(base + k * LANES, LANES), LANES)
        for r in range(11):
            own_ref[r, pl.ds(k, 1), :] = gauss_ref[pl.ds(r, 1), cols]
    (a, b, c), pull = jax.vjp(conic, *[own_ref[r] for r in range(2, 10)])
    opacity = sigmoid(own_ref[10])
    sx, sy, sxx, sxy, syy, s0 = grads[:6]
    rows = [a * sx + b * sy, b * sx + c * sy]
    rows += list(pull((-0.5 * sxx, -sxy, -0.5 * syy)))
    rows.append(s0 * (1.0 - opacity))
    basis = harmonic_rows(view_ref, 0, 16)
    for k in range(lines):
        cols = pl.ds(k * LANES, LANES)
        for r in range(11):
            out_ref[pl.ds(r, 1), cols] = rows[r][k : k + 1]
        for ch in range(3):
            out_ref[pl.ds(11 + 16 * ch, 16), cols] = basis * grads[6 + ch][k : k + 1]


def kernel(
    cells, shares,
    gauss_in, lists_in, blocks_in, order_in, view_in, cot_in,
    image_ref, out_ref,
    gauss_ref, lists_ref, blocks_ref, order_ref, view_ref, cot_ref, load_sem,
    rows_ref, table_ref, picked_ref, tri_ref, ratio_ref, weight_ref, parts_ref, logs_ref, tint_ref, seen_ref,
    grads_ref, spread_ref, hot_ref, share_ref, came_ref, own_ref,
    cell_send, cell_recv, tile_send, tile_recv,
):
    me = lax.axis_index("cell")
    row_of_tile = lax.axis_index("tile")
    chunk = gauss_ref.shape[1] // CHUNKS
    pairs = [(view_in, view_ref)]
    pairs += [
        (gauss_in.at[:, pl.ds(n * chunk, chunk)], gauss_ref.at[:, pl.ds(n * chunk, chunk)])
        for n in range(CHUNKS)
    ]
    pairs += [(lists_in, lists_ref), (blocks_in, blocks_ref), (cot_in, cot_ref), (order_in, order_ref)]
    loads = [pltpu.make_async_copy(src, dst, load_sem.at[n]) for n, (src, dst) in enumerate(pairs)]
    for load in loads:
        load.start()
    barrier = pltpu.get_barrier_semaphore()
    cell_peers = [lax.rem(me + off, cells) for off in range(1, cells)]
    tile_peers = [lax.rem(row_of_tile + off, shares) for off in range(1, shares)]
    for peer in cell_peers:
        pl.semaphore_signal(barrier, inc=1, device_id=(peer, row_of_tile), device_id_type=MESH)
    for peer in tile_peers:
        pl.semaphore_signal(barrier, inc=1, device_id=(me, peer), device_id_type=MESH)

    triangles(tri_ref)
    loads[0].wait()
    project_all(gauss_ref, view_ref, rows_ref, table_ref, loads[1 : 1 + CHUNKS])
    for load in loads[1 + CHUNKS :]:
        load.wait()
    gather_all(lists_ref, blocks_ref, table_ref, picked_ref)
    forward(me, picked_ref, tri_ref, ratio_ref, weight_ref, parts_ref, logs_ref, seen_ref)
    pl.semaphore_wait(barrier, cells + shares - 2)
    copies = []
    for n, peer in enumerate(cell_peers):
        copy = pltpu.make_async_remote_copy(
            src_ref=seen_ref.at[me], dst_ref=seen_ref.at[me],
            send_sem=cell_send.at[n], recv_sem=cell_recv.at[n],
            device_id=(peer, row_of_tile), device_id_type=MESH,
        )
        copy.start()
        copies.append(copy)
    for copy in copies:
        copy.wait()

    shape = seen_ref.shape[2:]
    light = [jnp.full(shape, BACKGROUND, F32) for _ in range(3)]
    behind = [jnp.zeros(shape, F32) for _ in range(3)]
    ahead = jnp.ones(shape, F32)
    passed = jnp.zeros(shape, jnp.int32)
    for s in reversed(range(cells)):
        cell = order_ref[s]
        mine = jnp.full(shape, cell, jnp.int32) == me
        kept = seen_ref[cell, 3]
        ahead = jnp.where(passed == 1, ahead * kept, ahead)
        for ch in range(3):
            behind[ch] = jnp.where(mine, light[ch], behind[ch])
            light[ch] = seen_ref[cell, ch] + kept * light[ch]
        passed = jnp.where(mine, 1, passed)
    after = jnp.zeros(shape, F32)
    for ch in range(3):
        image_ref[ch] = light[ch]
        tint = ahead * cot_ref[ch]
        tint_ref[ch] = tint
        after = after + tint * behind[ch]
    tint_ref[3] = after * seen_ref[me, 3]

    backward(picked_ref, tri_ref, ratio_ref, weight_ref, parts_ref, logs_ref, tint_ref, grads_ref)
    scatter_all(lists_ref, grads_ref, spread_ref, hot_ref, share_ref, table_ref.shape[1])
    copies = []
    for n, peer in enumerate(tile_peers):
        copy = pltpu.make_async_remote_copy(
            src_ref=share_ref.at[peer], dst_ref=came_ref.at[n],
            send_sem=tile_send.at[n], recv_sem=tile_recv.at[n],
            device_id=(me, peer), device_id_type=MESH,
        )
        copy.start()
        copies.append(copy)
    for copy in copies:
        copy.wait()
    grads = []
    for r in range(9):
        value = share_ref[row_of_tile, r]
        for n in range(shares - 1):
            value = value + came_ref[n, r]
        grads.append(value)
    pull_back(gauss_ref, view_ref, own_ref, grads, out_ref)


def solution(mesh):
    cells, shares = mesh.shape["cell"], mesh.shape["tile"]

    def on_device(gaussians, tile_lists, list_blocks, cell_order, view_vector, cotangent):
        tiles, length = tile_lists.shape[1:]
        pixels = cotangent.shape[2]
        count = gaussians.shape[1]
        blocks = count // LANES
        lines = blocks // shares
        vmem = pl.BlockSpec(memory_space=pltpu.VMEM)
        return pl.pallas_call(
            functools.partial(kernel, cells, shares),
            name="splat_step",
            out_shape=(
                jax.ShapeDtypeStruct(cotangent.shape, F32),
                jax.ShapeDtypeStruct((gaussians.shape[0], count // shares), F32),
            ),
            in_specs=[pl.BlockSpec(memory_space=pl.ANY)] * 6,
            out_specs=(vmem, vmem),
            scratch_shapes=[
                pltpu.VMEM(gaussians.shape, F32),
                pltpu.VMEM(tile_lists.shape, jnp.int32),
                pltpu.SMEM(list_blocks.shape, jnp.int32),
                pltpu.SMEM(cell_order.shape, jnp.int32),
                pltpu.SMEM(view_vector.shape, F32),
                pltpu.VMEM(cotangent.shape, F32),
                pltpu.SemaphoreType.DMA((CHUNKS + 5,)),
                pltpu.VMEM((11, blocks, LANES), F32),
                pltpu.VMEM((9, blocks, LANES), F32),
                pltpu.VMEM((9, tiles, length), F32),
                pltpu.VMEM((2, length, length), jnp.bfloat16),
                pltpu.VMEM((tiles, pixels, length), F32),
                pltpu.VMEM((tiles, pixels, length), F32),
                pltpu.VMEM((tiles, 2, pixels, length), jnp.bfloat16),
                pltpu.VMEM((4, pixels, length), jnp.bfloat16),
                pltpu.VMEM((4, tiles, pixels), F32),
                pltpu.VMEM((cells, 4, tiles, pixels), F32),
                pltpu.VMEM((9, tiles, length), F32),
                pltpu.VMEM((2, 9 * blocks, tiles * length), jnp.bfloat16),
                pltpu.VMEM((LANES, tiles * length), jnp.bfloat16),
                pltpu.VMEM((shares, 9, lines, LANES), F32),
                pltpu.VMEM((shares - 1, 9, lines, LANES), F32),
                pltpu.VMEM((11, lines, LANES), F32),
                pltpu.SemaphoreType.DMA((cells - 1,)),
                pltpu.SemaphoreType.DMA((cells - 1,)),
                pltpu.SemaphoreType.DMA((shares - 1,)),
                pltpu.SemaphoreType.DMA((shares - 1,)),
            ],
            compiler_params=pltpu.CompilerParams(
                collective_id=0, has_side_effects=True, vmem_limit_bytes=60 * 1024 * 1024
            ),
        )(gaussians, tile_lists, list_blocks, cell_order, view_vector, cotangent)

    placed = (
        P(None, "cell"),
        P("cell", "tile", None),
        P("cell", "tile"),
        P(),
        P(),
        P(None, "tile", None),
    )
    return jax.shard_map(
        on_device,
        mesh=mesh,
        in_specs=placed,
        out_specs=(P(None, "tile", None), P(None, ("cell", "tile"))),
        check_vma=False,
    )
```

profile of v0, /device:TPU:0, one launch (start us, length us, event | category | flops | bytes accessed | tf_op | source)
XLA Modules:
  0.0 29.1 jit_solution(438582757665305259)
XLA Ops:
  0.6 25.4 %splat_step.1 = (f32[3,8,256]{2,1,0:T(8,128)}, f32[59,1024]{1,0:T(8,128)}) custom-call(f32[59,4096]{1,0:T(8,128)} %gauss_in.1, s32[1,8,256]{2,1,0:T(8,128)} %lists_in.1, s32[1,8]{1,0:T(1,128)} %blocks_in.1, s32[8]{0:T(128)} %order_in.1, f32[3]{0:T(128)} %view_in.1, f32[3,8,256]{2,1,0:T(8,128)} %cot_in.1), custom_call_target="tpu_custom_call" | custom-call | tf_op jit(solution)/shard_map/splat_step/pallas_call | solution.py:417
  26.0 1.3 %copy.10 = f32[3,8,256]{2,1,0:T(8,128)} copy(f32[3,8,256]{2,1,0:T(8,128)} %get-tuple-element.4) | data formatting | bytes 49152
  27.4 1.7 %copy.11 = f32[59,1024]{1,0:T(8,128)} copy(f32[59,1024]{1,0:T(8,128)} %get-tuple-element.5) | data formatting | bytes 483328
where the time goes:
time: 29.3 us; the launch traced here: 29.1 us
  Pallas kernels  25.4 us (87%)
  local copies, waits for them, and re-layouts  3.02 us (10%)
  between operations  0.64 us (2%)
    pallas_call x1, Pallas kernels, on_device(): pl.pallas_call(functools.partial(kernel, cells, shares), name='splat_step...  25.4 us
    unnamed x2, local copies, waits for them, and re-layouts  3.02 us

commit v1 on v0

--- a/solution.py
+++ b/solution.py
@@ -404,6 +404,11 @@
     pull_back(gauss_ref, view_ref, own_ref, grads, out_ref)
 
 
+def finish(image_in, rows_in, image_ref, rows_ref):
+    image_ref[...] = image_in[...]
+    rows_ref[...] = rows_in[...]
+
+
 def solution(mesh):
     cells, shares = mesh.shape["cell"], mesh.shape["tile"]
 
@@ -414,7 +419,7 @@
         blocks = count // LANES
         lines = blocks // shares
         vmem = pl.BlockSpec(memory_space=pltpu.VMEM)
-        return pl.pallas_call(
+        image, rows = pl.pallas_call(
             functools.partial(kernel, cells, shares),
             name="splat_step",
             out_shape=(
@@ -453,9 +458,23 @@
                 pltpu.SemaphoreType.DMA((shares - 1,)),
             ],
             compiler_params=pltpu.CompilerParams(
-                collective_id=0, has_side_effects=True, vmem_limit_bytes=60 * 1024 * 1024
+                collective_id=0, has_side_effects=True, vmem_limit_bytes=24 * 1024 * 1024
             ),
-        )(gaussians, tile_lists, list_blocks, cell_order, view_vector, cotangent)
+        )(*[
+            pltpu.with_memory_space_constraint(x, pltpu.HBM)
+            for x in (gaussians, tile_lists, list_blocks, cell_order, view_vector, cotangent)
+        ])
+        return pl.pallas_call(
+            finish,
+            name="finish",
+            out_shape=(
+                jax.ShapeDtypeStruct(image.shape, F32),
+                jax.ShapeDtypeStruct(rows.shape, F32),
+            ),
+            in_specs=[vmem] * 2,
+            out_specs=(vmem, vmem),
+            compiler_params=pltpu.CompilerParams(vmem_limit_bytes=4 * 1024 * 1024),
+        )(image, rows)
 
     placed = (
         P(None, "cell"),

time: 29.3 us -> 26.2 us (0.89)
  local copies, waits for them, and re-layouts: 3.02 us -> 0 us
    unnamed x2 -> x0, local copies, waits for them, and re-layouts: 3.02 us -> none
    pallas_call x0 -> x1, Pallas kernels: none -> 0.73 us  [on_device(): pl.pallas_call(finish, name='finish', out_shape=(jax.ShapeDtypeStruct(ima...]
    pallas_call x1, Pallas kernels: 25.4 us -> 24.7 us  [on_device(): pl.pallas_call(functools.partial(kernel, cells, shares), name='splat_step...]
where the time goes in v1:
time: 26.2 us; the launch traced here: 26.1 us
  Pallas kernels  25.4 us (97%)
  between operations  0.64 us (2%)
    pallas_call x1, Pallas kernels, on_device(): pl.pallas_call(functools.partial(kernel, cells, shares), name='splat_step...  24.7 us
    pallas_call x1, Pallas kernels, on_device(): pl.pallas_call(finish, name='finish', out_shape=(jax.ShapeDtypeStruct(ima...  0.73 us

profile of v1, /device:TPU:0, one launch (start us, length us, event | category | flops | bytes accessed | tf_op | source)
XLA Modules:
  0.0 26.1 jit_solution(2886001531860164319)
XLA Ops:
  0.6 24.7 %splat_step.1 = (f32[3,8,256]{2,1,0:T(8,128)S(1)}, f32[59,1024]{1,0:T(8,128)S(1)}) custom-call(f32[59,4096]{1,0:T(8,128)} %gauss_in.1, s32[1,8,256]{2,1,0:T(8,128)} %lists_in.1, s32[1,8]{1,0:T(1,128)} %blocks_in.1, s32[8]{0:T(128)} %order_in.1, f32[3]{0:T(128)} %view_in.1, f32[3,8,256]{2,1,0:T(8,128)} %cot_in.1), custom_call_target="tpu_custom_call" | custom-call | tf_op jit(solution)/shard_map/splat_step/pallas_call | solution.py:422
  25.3 0.7 %finish.1 = (f32[3,8,256]{2,1,0:T(8,128)}, f32[59,1024]{1,0:T(8,128)}) custom-call(f32[3,8,256]{2,1,0:T(8,128)S(1)} %get-tuple-element.4.image_in, f32[59,1024]{1,0:T(8,128)S(1)} %get-tuple-element.5.rows_in), custom_call_target="tpu_custom_call" | custom-call | tf_op jit(solution)/shard_map/finish/pallas_call | solution.py:467

commit v2 on v1

v2 whole, which is shorter than its diff:
```python
import functools

import jax
import jax.numpy as jnp
from jax import lax
from jax.experimental import pallas as pl
from jax.experimental.pallas import tpu as pltpu
from jax.sharding import PartitionSpec as P

TILE_SIDE = 16
LANES = 128
CHUNKS = 4
UNROLL = 2
ROWS = 16
SUBLANES = 8
WIDE = 256
FORM_ROWS = 32
NOTHING = -1e9
LOG2E = 1.4426950408889634
BACKGROUND = 1.0
FOCAL = 6.0
BLUR = 0.3
F32 = jnp.float32
MESH = pl.DeviceIdType.MESH


def harmonic_basis(vx, vy, vz):
    norm = jnp.sqrt(vx * vx + vy * vy + vz * vz)
    x, y, z = vx / norm, vy / norm, vz / norm
    return [
        0.28209479177387814 + 0.0 * x,
        -0.4886025119029199 * y,
        0.4886025119029199 * z,
        -0.4886025119029199 * x,
        1.0925484305920792 * x * y,
        -1.0925484305920792 * y * z,
        0.31539156525252005 * (2.0 * z * z - x * x - y * y),
        -1.0925484305920792 * x * z,
        0.5462742152960396 * (x * x - y * y),
        -0.5900435899266435 * y * (3.0 * x * x - y * y),
        2.890611442640554 * x * y * z,
        -0.4570457994644658 * y * (4.0 * z * z - x * x - y * y),
        0.3731763325901154 * z * (2.0 * z * z - 3.0 * x * x - 3.0 * y * y),
        -0.4570457994644658 * x * (4.0 * z * z - x * x - y * y),
        1.445305721320277 * z * (x * x - y * y),
        -0.5900435899266435 * x * (x * x - 3.0 * y * y),
    ]


def conic(depth, s0, s1, s2, q0, q1, q2, q3):
    scales = [jnp.exp(2.0 * s) for s in (s0, s1, s2)]
    norm = jnp.sqrt(q0 * q0 + q1 * q1 + q2 * q2 + q3 * q3)
    w, a, b, c = q0 / norm, q1 / norm, q2 / norm, q3 / norm
    row_one = (1.0 - 2.0 * (b * b + c * c), 2.0 * (a * b - w * c), 2.0 * (a * c + w * b))
    row_two = (2.0 * (a * b + w * c), 1.0 - 2.0 * (a * a + c * c), 2.0 * (b * c - w * a))
    ratio = FOCAL / depth
    zoom = ratio * ratio
    xx = zoom * sum(row_one[k] * row_one[k] * scales[k] for k in range(3)) + BLUR
    xy = zoom * sum(row_one[k] * row_two[k] * scales[k] for k in range(3))
    yy = zoom * sum(row_two[k] * row_two[k] * scales[k] for k in range(3)) + BLUR
    det = xx * yy - xy * xy
    return yy / det, -xy / det, xx / det


def sigmoid(x):
    return 1.0 / (1.0 + jnp.exp(-x))


def pick(values, lane):
    return jnp.take_along_axis(values, lane, axis=1, mode="promise_in_bounds")


def harmonic_rows(view_ref, first, rows):
    shape = (rows, LANES)
    vx, vy, vz = (jnp.full(shape, view_ref[k], F32) for k in range(3))
    row = lax.broadcasted_iota(jnp.int32, shape, 0)
    out = jnp.zeros(shape, F32)
    for k, value in enumerate(harmonic_basis(vx, vy, vz)):
        out = jnp.where(row == first + k, value, out)
    return out


def project_all(gauss_ref, view_ref, rows_ref, table_ref, loads):
    blocks = gauss_ref.shape[1] // LANES
    weights = harmonic_rows(view_ref, 3, 24)
    for k in range(blocks):
        if k % (blocks // CHUNKS) == 0:
            loads[k // (blocks // CHUNKS)].wait()
        cols = pl.ds(k * LANES, LANES)
        for r in range(11):
            rows_ref[r, pl.ds(k, 1), :] = gauss_ref[pl.ds(r, 1), cols]
        for ch in range(3):
            start = 8 + 16 * ch
            size = min(24, gauss_ref.shape[0] - start)
            part = gauss_ref[pl.ds(start, size), cols] * weights[:size]
            table_ref[6 + ch, pl.ds(k, 1), :] = 0.5 + jnp.sum(part, axis=0, keepdims=True)
    a, b, c = conic(*[rows_ref[r] for r in range(2, 10)])
    table_ref[0] = rows_ref[0]
    table_ref[1] = rows_ref[1]
    table_ref[2] = a
    table_ref[3] = b
    table_ref[4] = c
    table_ref[5] = sigmoid(rows_ref[10])


def entry_of(part, length):
    at = lax.broadcasted_iota(jnp.int32, (SUBLANES, LANES), 1) + part * LANES
    return (at % SUBLANES) * (length // SUBLANES) + at // SUBLANES


def gather_all(lists_ref, blocks_ref, table_ref, index_ref, picked_ref):
    tiles, length = lists_ref.shape[1], lists_ref.shape[2]
    shape = (tiles, LANES)
    row = lax.broadcasted_iota(jnp.int32, shape, 0)
    limit = jnp.zeros(shape, jnp.int32)
    for t in range(tiles):
        limit = jnp.where(row == t, blocks_ref[0, t] * LANES, limit)
    row_of_tile = lax.axis_index("tile")
    centre_x = (row * TILE_SIDE + TILE_SIDE // 2).astype(F32)
    centre_y = jnp.full(shape, row_of_tile * TILE_SIDE + TILE_SIDE // 2, jnp.int32).astype(F32)
    for part in range(length // LANES):
        cols = pl.ds(part * LANES, LANES)
        entry = jnp.broadcast_to(entry_of(part, length)[:1], shape)
        index = jnp.zeros(shape, jnp.int32)
        for source in range(length // LANES):
            moved = pick(lists_ref[0, :, pl.ds(source * LANES, LANES)], entry % LANES)
            index = jnp.where(entry // LANES == source, moved, index)
        index_ref[:, cols] = index
        high = index // LANES
        low = index - high * LANES
        values = [jnp.zeros(shape, F32) for _ in range(9)]
        for k in range(table_ref.shape[1]):
            hit = high == k
            for r in range(9):
                line = jnp.broadcast_to(table_ref[r, pl.ds(k, 1), :], shape)
                values[r] = jnp.where(hit, pick(line, low), values[r])
        values[0] = values[0] - centre_x
        values[1] = values[1] - centre_y
        values[5] = jnp.where(entry < limit, values[5], 0.0)
        for r in range(9):
            picked_ref[r, :, cols] = values[r]


def split(value):
    top = value.astype(jnp.bfloat16)
    return top, (value - top.astype(F32)).astype(jnp.bfloat16)


def dot(a, b):
    return jnp.dot(a, b, preferred_element_type=F32)


def dot_rows(a, b):
    return lax.dot_general(a, b, (((1,), (1,)), ((), ())), preferred_element_type=F32)


def dot_columns(a, b):
    return lax.dot_general(a, b, (((0,), (0,)), ((), ())), preferred_element_type=F32)


def pieces(value, count):
    out = []
    for _ in range(count):
        top = value.astype(jnp.bfloat16).astype(F32)
        out.append(top)
        value = value - top
    return out


def set_rows(ref, tiles, first, values):
    for n, value in enumerate(values):
        for part in range(ref.shape[0]):
            ref[part, pl.ds((first + n) * tiles, tiles), :] = value[:, part * LANES : (part + 1) * LANES]


def rows_of(ref, t, count, tiles):
    halves = [ref.at[part][pl.ds(t, count, stride=tiles), :] for part in range(ref.shape[0])]
    return jnp.concatenate(halves, axis=1).astype(jnp.bfloat16)


def pixel_basis(basis_ref):
    shape = basis_ref.shape
    pixel = lax.broadcasted_iota(jnp.int32, shape, 1)
    row = lax.broadcasted_iota(jnp.int32, shape, 0)
    half = 0.5 * (TILE_SIDE - 1)
    px = (pixel % TILE_SIDE).astype(F32) - half
    py = (pixel // TILE_SIDE).astype(F32) - half
    out = jnp.zeros(shape, F32)
    for n, value in enumerate([jnp.ones_like(px), px, py, px * px, px * py, py * py]):
        out = jnp.where((row % 6 == n) & (row < 18), value, out)
    basis_ref[...] = out.astype(jnp.bfloat16)


def form_all(picked_ref, cot_ref, form_ref, glow_ref):
    tiles = picked_ref.shape[1]
    cx, cy, a, b, c, op = (picked_ref[r] for r in range(6))
    sx = a * cx + b * cy
    sy = b * cx + c * cy
    level = jnp.where(op > 0.0, jnp.log(jnp.maximum(op, 1e-37)), NOTHING)
    forms = [level - 0.5 * (cx * sx + cy * sy), sx, sy, -0.5 * a, -b, -0.5 * c]
    forms = [pieces(value * LOG2E, 3) for value in forms]
    for p in range(3):
        set_rows(form_ref, tiles, 6 * p, [form[p] for form in forms])
    tints = [pieces(picked_ref[6 + ch], 2) for ch in range(3)]
    for n, p in enumerate((0, 0, 1)):
        set_rows(form_ref, tiles, 18 + 3 * n, [tint[p] for tint in tints])
    set_rows(form_ref, tiles, 27, [jnp.zeros_like(cx)] * 5)
    cots = [pieces(cot_ref[ch], 2) for ch in range(3)]
    blank = jnp.zeros_like(cot_ref[0])
    set_rows(glow_ref, tiles, 0, [blank] * 18)
    for n, p in enumerate((0, 1, 0)):
        set_rows(glow_ref, tiles, 18 + 3 * n, [cot[p] for cot in cots])
    set_rows(glow_ref, tiles, 27, [blank] * 5)


def forward(me, form_ref, basis_ref, alpha_ref, weight_ref, parts_ref, crit_ref, tone_ref):
    tiles, length, pixels = alpha_ref.shape
    shape = (SUBLANES, pixels)
    line = lax.broadcasted_iota(jnp.int32, shape, 0)

    def one_tile(t, _):
        form = rows_of(form_ref, t, FORM_ROWS, tiles)
        level = dot_columns(form, basis_ref[...])
        through = jnp.ones(shape, F32)
        for v in range(length // SUBLANES):
            rows = pl.ds(v * SUBLANES, SUBLANES)
            alpha = jnp.exp2(level[v * SUBLANES : (v + 1) * SUBLANES])
            alpha_ref[t, rows, :] = alpha
            weight = alpha * through
            weight_ref[t, rows, :] = weight
            through = through - weight
        for d in (1, 2, 4):
            through = jnp.where(line >= d, through * pltpu.roll(through, d, 0), through)
        crit_ref[me, 0, pl.ds(t, 1), :] = through[SUBLANES - 1 :]
        ahead = jnp.where(line >= 1, pltpu.roll(through, 1, 0), 1.0)
        ahead = jnp.concatenate([ahead, ahead], axis=0)
        for v in range(length // ROWS):
            rows = pl.ds(v * ROWS, ROWS)
            weight = weight_ref[t, rows, :] * ahead
            weight_ref[t, rows, :] = weight
            top, rest = split(weight)
            parts_ref[t, 0, rows, :] = top
            parts_ref[t, 1, rows, :] = rest
        tint = form[FORM_ROWS - ROWS :]
        colour = dot(tint, parts_ref[t, 0]) + dot(tint, parts_ref[t, 1])
        skip = 18 - (FORM_ROWS - ROWS)
        for ch in range(3):
            tone_ref[me, ch, pl.ds(t, 1), :] = colour[skip + ch : skip + ch + 1] + colour[skip + 6 + ch : skip + 7 + ch]
        return 0

    lax.fori_loop(0, tiles, one_tile, 0, unroll=UNROLL)


def local_backward(form_ref, glow_ref, alpha_ref, weight_ref, ends_ref):
    tiles, length, pixels = alpha_ref.shape
    shape = (SUBLANES, pixels)
    line = lax.broadcasted_iota(jnp.int32, shape, 0)

    def one_tile(t, _):
        light = dot_columns(rows_of(form_ref, t, FORM_ROWS, tiles), rows_of(glow_ref, t, FORM_ROWS, tiles))
        seen = jnp.zeros(shape, F32)
        keep = jnp.ones(shape, F32)
        for v in reversed(range(length // SUBLANES)):
            rows = pl.ds(v * SUBLANES, SUBLANES)
            alpha = alpha_ref[t, rows, :]
            weight = weight_ref[t, rows, :]
            change = light[v * SUBLANES : (v + 1) * SUBLANES] - seen
            alpha_ref[t, rows, :] = weight * change
            weight_ref[t, rows, :] = weight * keep
            seen = seen + alpha * change
            keep = keep - alpha * keep
        for d in (1, 2, 4):
            inside = line < SUBLANES - d
            seen = jnp.where(inside, seen + keep * pltpu.roll(seen, SUBLANES - d, 0), seen)
            keep = jnp.where(inside, keep * pltpu.roll(keep, SUBLANES - d, 0), keep)
        inside = line < SUBLANES - 1
        ends_ref[t, 0] = jnp.where(inside, pltpu.roll(seen, SUBLANES - 1, 0), 0.0)
        ends_ref[t, 1] = jnp.where(inside, pltpu.roll(keep, SUBLANES - 1, 0), 1.0)
        return 0

    lax.fori_loop(0, tiles, one_tile, 0, unroll=UNROLL)


def mark_all(index_ref, hot_ref, hit_ref):
    tiles, length = index_ref.shape
    low_size, blocks = hot_ref.shape[0], hit_ref.shape[0]
    for t in range(tiles):
        index = index_ref[pl.ds(t, 1), :]
        high = index // low_size
        low = index - high * low_size
        cols = pl.ds(t * length, length)
        line = lax.broadcasted_iota(jnp.int32, (low_size, length), 0)
        hot_ref[:, cols] = jnp.where(line == low, 1.0, 0.0).astype(jnp.bfloat16)
        hit_ref[:, cols] = jnp.where(lax.broadcasted_iota(jnp.int32, (blocks, length), 0) == high, 1.0, 0.0)


def backward(basis_ref, alpha_ref, weight_ref, parts_ref, ends_ref, scene_ref, tint_ref, slope_ref, moments_ref):
    tiles, length, pixels = alpha_ref.shape
    basis = basis_ref[:ROWS]

    def one_tile(t, _):
        ahead = scene_ref[0, pl.ds(t, 1), :]
        behind = scene_ref[1, pl.ds(t, 1), :]
        under = ahead * (ends_ref[t, 0] + ends_ref[t, 1] * behind)
        under = jnp.concatenate([under, under], axis=0)
        for v in range(length // ROWS):
            rows = pl.ds(v * ROWS, ROWS)
            top, rest = split(ahead * alpha_ref[t, rows, :] - under * weight_ref[t, rows, :])
            slope_ref[t, 0, rows, :] = top
            slope_ref[t, 1, rows, :] = rest
        sums = dot_rows(basis, slope_ref[t, 0]) + dot_rows(basis, slope_ref[t, 1])
        tint = rows_of(tint_ref, t, ROWS, tiles)
        colour = dot_rows(tint, parts_ref[t, 0]) + dot_rows(tint, parts_ref[t, 1])
        here = pl.ds(t, 1)
        for n in range(6):
            moments_ref[n, here, :] = sums[n : n + 1]
        for ch in range(3):
            moments_ref[6 + ch, here, :] = colour[ch : ch + 1] + colour[3 + ch : 4 + ch]
        return 0

    lax.fori_loop(0, tiles, one_tile, 0, unroll=UNROLL)


def scatter_all(picked_ref, moments_ref, grads_ref, spread_ref, hot_ref, hit_ref, share_ref):
    tiles, length = moments_ref.shape[1], moments_ref.shape[2]
    blocks = hit_ref.shape[0]
    cx, cy = picked_ref[0], picked_ref[1]
    m0, mx, my, mxx, mxy, myy = (moments_ref[n] for n in range(6))
    grads_ref[0] = mx - cx * m0
    grads_ref[1] = my - cy * m0
    grads_ref[2] = mxx - 2.0 * cx * mx + cx * cx * m0
    grads_ref[3] = mxy - cx * my - cy * mx + cx * cy * m0
    grads_ref[4] = myy - 2.0 * cy * my + cy * cy * m0
    grads_ref[5] = m0
    for ch in range(3):
        grads_ref[6 + ch] = moments_ref[6 + ch]
    for t in range(tiles):
        cols = pl.ds(t * length, length)
        hit = hit_ref[:, cols]
        for r in range(9):
            top, rest = split(hit * grads_ref[r, pl.ds(t, 1), :])
            rows = pl.ds(r * blocks, blocks)
            spread_ref[0, rows, cols] = top
            spread_ref[1, rows, cols] = rest
    hot = hot_ref[...]
    total = dot_rows(spread_ref[0], hot) + dot_rows(spread_ref[1], hot)
    shares, _, lines, _ = share_ref.shape
    for s in range(shares):
        for r in range(9):
            share_ref[s, r] = total[r * blocks + s * lines : r * blocks + (s + 1) * lines]


def pull_back(gauss_ref, view_ref, own_ref, grads, out_ref):
    lines, width = own_ref.shape[1:]
    base = lax.axis_index("tile") * (lines * width)
    for k in range(lines):
        cols = pl.ds(pl.multiple_of(base + k * width, width), width)
        for r in range(11):
            own_ref[r, pl.ds(k, 1), :] = gauss_ref[pl.ds(r, 1), cols]
    (a, b, c), pull = jax.vjp(conic, *[own_ref[r] for r in range(2, 10)])
    opacity = sigmoid(own_ref[10])
    sx, sy, sxx, sxy, syy, s0 = grads[:6]
    rows = [a * sx + b * sy, b * sx + c * sy]
    rows += list(pull((-0.5 * sxx, -sxy, -0.5 * syy)))
    rows.append(s0 * (1.0 - opacity))
    basis = jnp.concatenate([harmonic_rows(view_ref, 0, 16)] * (width // LANES), axis=1)
    for k in range(lines):
        cols = pl.ds(k * width, width)
        for r in range(11):
            out_ref[pl.ds(r, 1), cols] = rows[r][k : k + 1]
        for ch in range(3):
            out_ref[pl.ds(11 + 16 * ch, 16), cols] = basis * grads[6 + ch][k : k + 1]


def kernel(
    cells, shares,
    gauss_in, lists_in, blocks_in, order_in, view_in, cot_in,
    image_ref, out_ref,
    gauss_ref, lists_ref, blocks_ref, order_ref, view_ref, cot_ref, load_sem,
    rows_ref, table_ref, index_ref, picked_ref, form_ref, glow_ref, basis_ref, alpha_ref, weight_ref, parts_ref, slope_ref,
    ends_ref, scene_ref, tint_ref, crit_ref, tone_ref, moments_ref, grads_ref, spread_ref, hot_ref, hit_ref,
    share_ref, came_ref, own_ref,
    crit_send, crit_recv, tone_send, tone_recv, tile_send, tile_recv,
):
    me = lax.axis_index("cell")
    row_of_tile = lax.axis_index("tile")
    chunk = gauss_ref.shape[1] // CHUNKS
    pairs = [(view_in, view_ref)]
    pairs += [
        (gauss_in.at[:, pl.ds(n * chunk, chunk)], gauss_ref.at[:, pl.ds(n * chunk, chunk)])
        for n in range(CHUNKS)
    ]
    pairs += [(lists_in, lists_ref), (blocks_in, blocks_ref), (cot_in, cot_ref), (order_in, order_ref)]
    loads = [pltpu.make_async_copy(src, dst, load_sem.at[n]) for n, (src, dst) in enumerate(pairs)]
    for load in loads:
        load.start()
    barrier = pltpu.get_barrier_semaphore()
    cell_peers = [lax.rem(me + off, cells) for off in range(1, cells)]
    tile_peers = [lax.rem(row_of_tile + off, shares) for off in range(1, shares)]
    for peer in cell_peers:
        pl.semaphore_signal(barrier, inc=1, device_id=(peer, row_of_tile), device_id_type=MESH)
    for peer in tile_peers:
        pl.semaphore_signal(barrier, inc=1, device_id=(me, peer), device_id_type=MESH)

    pixel_basis(basis_ref)
    loads[0].wait()
    project_all(gauss_ref, view_ref, rows_ref, table_ref, loads[1 : 1 + CHUNKS])
    for load in loads[1 + CHUNKS :]:
        load.wait()
    gather_all(lists_ref, blocks_ref, table_ref, index_ref, picked_ref)
    form_all(picked_ref, cot_ref, form_ref, glow_ref)
    forward(me, form_ref, basis_ref, alpha_ref, weight_ref, parts_ref, crit_ref, tone_ref)
    crit_ref[me, 1] = sum(cot_ref[ch] * tone_ref[me, ch] for ch in range(3))
    pl.semaphore_wait(barrier, cells + shares - 2)
    groups = []
    for ref, send, recv in ((crit_ref, crit_send, crit_recv), (tone_ref, tone_send, tone_recv)):
        copies = []
        for n, peer in enumerate(cell_peers):
            copy = pltpu.make_async_remote_copy(
                src_ref=ref.at[me], dst_ref=ref.at[me],
                send_sem=send.at[n], recv_sem=recv.at[n],
                device_id=(peer, row_of_tile), device_id_type=MESH,
            )
            copy.start()
            copies.append(copy)
        groups.append(copies)
    local_backward(form_ref, glow_ref, alpha_ref, weight_ref, ends_ref)
    mark_all(index_ref, hot_ref, hit_ref)
    for copy in groups[0]:
        copy.wait()

    shape = crit_ref.shape[2:]
    light = BACKGROUND * (cot_ref[0] + cot_ref[1] + cot_ref[2])
    behind = jnp.zeros(shape, F32)
    ahead = jnp.ones(shape, F32)
    passed = jnp.zeros(shape, jnp.int32)
    for s in reversed(range(cells)):
        cell = order_ref[s]
        mine = jnp.full(shape, cell, jnp.int32) == me
        kept = crit_ref[cell, 0]
        ahead = jnp.where(passed == 1, ahead * kept, ahead)
        behind = jnp.where(mine, light, behind)
        light = crit_ref[cell, 1] + kept * light
        passed = jnp.where(mine, 1, passed)
    scene_ref[0] = ahead
    scene_ref[1] = behind
    tints = [pieces(ahead * cot_ref[ch], 2) for ch in range(3)]
    for p in range(2):
        set_rows(tint_ref, shape[0], 3 * p, [tint[p] for tint in tints])
    set_rows(tint_ref, shape[0], 6, [jnp.zeros(shape, F32)] * (ROWS - 6))

    backward(basis_ref, alpha_ref, weight_ref, parts_ref, ends_ref, scene_ref, tint_ref, slope_ref, moments_ref)
    scatter_all(picked_ref, moments_ref, grads_ref, spread_ref, hot_ref, hit_ref, share_ref)
    copies = []
    for n, peer in enumerate(tile_peers):
        copy = pltpu.make_async_remote_copy(
            src_ref=share_ref.at[peer], dst_ref=came_ref.at[n],
            send_sem=tile_send.at[n], recv_sem=tile_recv.at[n],
            device_id=(me, peer), device_id_type=MESH,
        )
        copy.start()
        copies.append(copy)
    for copy in groups[1]:
        copy.wait()
    image = [jnp.full(shape, BACKGROUND, F32) for _ in range(3)]
    for s in reversed(range(cells)):
        cell = order_ref[s]
        kept = crit_ref[cell, 0]
        for ch in range(3):
            image[ch] = tone_ref[cell, ch] + kept * image[ch]
    for ch in range(3):
        image_ref[ch] = image[ch]
    for copy in copies:
        copy.wait()
    grads = []
    for r in range(9):
        value = share_ref[row_of_tile, r]
        for n in range(shares - 1):
            value = value + came_ref[n, r]
        grads.append(value)
    pull_back(gauss_ref, view_ref, own_ref, grads, out_ref)


def finish(image_in, rows_in, image_ref, rows_ref):
    image_ref[...] = image_in[...]
    rows_ref[...] = rows_in[...]


def solution(mesh):
    cells, shares = mesh.shape["cell"], mesh.shape["tile"]

    def on_device(gaussians, tile_lists, list_blocks, cell_order, view_vector, cotangent):
        tiles, length = tile_lists.shape[1:]
        pixels = cotangent.shape[2]
        count = gaussians.shape[1]
        blocks = count // LANES
        groups = count // WIDE
        lines = groups // shares
        vmem = pl.BlockSpec(memory_space=pltpu.VMEM)
        image, rows = pl.pallas_call(
            functools.partial(kernel, cells, shares),
            name="splat_step",
            out_shape=(
                jax.ShapeDtypeStruct(cotangent.shape, F32),
                jax.ShapeDtypeStruct((gaussians.shape[0], count // shares), F32),
            ),
            in_specs=[pl.BlockSpec(memory_space=pl.ANY)] * 6,
            out_specs=(vmem, vmem),
            scratch_shapes=[
                pltpu.VMEM(gaussians.shape, F32),
                pltpu.VMEM(tile_lists.shape, jnp.int32),
                pltpu.SMEM(list_blocks.shape, jnp.int32),
                pltpu.SMEM(cell_order.shape, jnp.int32),
                pltpu.SMEM(view_vector.shape, F32),
                pltpu.VMEM(cotangent.shape, F32),
                pltpu.SemaphoreType.DMA((CHUNKS + 5,)),
                pltpu.VMEM((11, blocks, LANES), F32),
                pltpu.VMEM((9, blocks, LANES), F32),
                pltpu.VMEM((tiles, length), jnp.int32),
                pltpu.VMEM((9, tiles, length), F32),
                pltpu.VMEM((length // LANES, FORM_ROWS * tiles, LANES), F32),
                pltpu.VMEM((pixels // LANES, FORM_ROWS * tiles, LANES), F32),
                pltpu.VMEM((FORM_ROWS, pixels), jnp.bfloat16),
                pltpu.VMEM((tiles, length, pixels), F32),
                pltpu.VMEM((tiles, length, pixels), F32),
                pltpu.VMEM((tiles, 2, length, pixels), jnp.bfloat16),
                pltpu.VMEM((tiles, 2, length, pixels), jnp.bfloat16),
                pltpu.VMEM((tiles, 2, SUBLANES, pixels), F32),
                pltpu.VMEM((2, tiles, pixels), F32),
                pltpu.VMEM((pixels // LANES, ROWS * tiles, LANES), F32),
                pltpu.VMEM((cells, 2, tiles, pixels), F32),
                pltpu.VMEM((cells, 3, tiles, pixels), F32),
                pltpu.VMEM((9, tiles, length), F32),
                pltpu.VMEM((9, tiles, length), F32),
                pltpu.VMEM((2, 9 * groups, tiles * length), jnp.bfloat16),
                pltpu.VMEM((WIDE, tiles * length), jnp.bfloat16),
                pltpu.VMEM((groups, tiles * length), F32),
                pltpu.VMEM((shares, 9, lines, WIDE), F32),
                pltpu.VMEM((shares - 1, 9, lines, WIDE), F32),
                pltpu.VMEM((11, lines, WIDE), F32),
                pltpu.SemaphoreType.DMA((cells - 1,)),
                pltpu.SemaphoreType.DMA((cells - 1,)),
                pltpu.SemaphoreType.DMA((cells - 1,)),
                pltpu.SemaphoreType.DMA((cells - 1,)),
                pltpu.SemaphoreType.DMA((shares - 1,)),
                pltpu.SemaphoreType.DMA((shares - 1,)),
            ],
            compiler_params=pltpu.CompilerParams(
                collective_id=0, has_side_effects=True, vmem_limit_bytes=24 * 1024 * 1024
            ),
        )(*[
            pltpu.with_memory_space_constraint(x, pltpu.HBM)
            for x in (gaussians, tile_lists, list_blocks, cell_order, view_vector, cotangent)
        ])
        return pl.pallas_call(
            finish,
            name="finish",
            out_shape=(
                jax.ShapeDtypeStruct(image.shape, F32),
                jax.ShapeDtypeStruct(rows.shape, F32),
            ),
            in_specs=[vmem] * 2,
            out_specs=(vmem, vmem),
            compiler_params=pltpu.CompilerParams(vmem_limit_bytes=4 * 1024 * 1024),
        )(image, rows)

    placed = (
        P(None, "cell"),
        P("cell", "tile", None),
        P("cell", "tile"),
        P(),
        P(),
        P(None, "tile", None),
    )
    return jax.shard_map(
        on_device,
        mesh=mesh,
        in_specs=placed,
        out_specs=(P(None, "tile", None), P(None, ("cell", "tile"))),
        check_vma=False,
    )
```

time: 26.2 us -> 21.3 us (0.81)
  the two profiles are of different devices: /device:TPU:0 before, /device:TPU:11 now
where the time goes in v2:
time: 21.3 us; the launch traced here: 21.1 us
  Pallas kernels  20.5 us (96%)
  between operations  0.64 us (3%)
    pallas_call x1, Pallas kernels, on_device(): pl.pallas_call(functools.partial(kernel, cells, shares), name='splat_step...  19.7 us
    pallas_call x1, Pallas kernels, on_device(): pl.pallas_call(finish, name='finish', out_shape=(jax.ShapeDtypeStruct(ima...  0.73 us

profile of v2, /device:TPU:11, one launch (start us, length us, event | category | flops | bytes accessed | tf_op | source)
XLA Modules:
  0.0 21.1 jit_solution(4567833198826354070)
XLA Ops:
  0.6 19.7 %splat_step.1 = (f32[3,8,256]{2,1,0:T(8,128)S(1)}, f32[59,1024]{1,0:T(8,128)S(1)}) custom-call(f32[59,4096]{1,0:T(8,128)} %gauss_in.1, s32[1,8,256]{2,1,0:T(8,128)} %lists_in.1, s32[1,8]{1,0:T(1,128)} %blocks_in.1, s32[8]{0:T(128)} %order_in.1, f32[3]{0:T(128)} %view_in.1, f32[3,8,256]{2,1,0:T(8,128)} %cot_in.1), custom_call_target="tpu_custom_call" | custom-call | tf_op jit(solution)/shard_map/splat_step/pallas_call | solution.py:500
  20.4 0.7 %finish.1 = (f32[3,8,256]{2,1,0:T(8,128)}, f32[59,1024]{1,0:T(8,128)}) custom-call(f32[3,8,256]{2,1,0:T(8,128)S(1)} %get-tuple-element.4.image_in, f32[59,1024]{1,0:T(8,128)S(1)} %get-tuple-element.5.rows_in), custom_call_target="tpu_custom_call" | custom-call | tf_op jit(solution)/shard_map/finish/pallas_call | solution.py:555

commit v3 on v2

--- a/solution.py
+++ b/solution.py
@@ -10,7 +10,7 @@
 TILE_SIDE = 16
 LANES = 128
 CHUNKS = 4
-UNROLL = 2
+UNROLL = 8
 ROWS = 16
 SUBLANES = 8
 WIDE = 256
@@ -220,13 +220,11 @@
 
     def one_tile(t, _):
         form = rows_of(form_ref, t, FORM_ROWS, tiles)
-        level = dot_columns(form, basis_ref[...])
+        alpha_ref[t] = jnp.exp2(dot_columns(form, basis_ref[...]))
         through = jnp.ones(shape, F32)
         for v in range(length // SUBLANES):
             rows = pl.ds(v * SUBLANES, SUBLANES)
-            alpha = jnp.exp2(level[v * SUBLANES : (v + 1) * SUBLANES])
-            alpha_ref[t, rows, :] = alpha
-            weight = alpha * through
+            weight = alpha_ref[t, rows, :] * through
             weight_ref[t, rows, :] = weight
             through = through - weight
         for d in (1, 2, 4):
@@ -340,10 +338,11 @@
         for r in range(9):
             top, rest = split(hit * grads_ref[r, pl.ds(t, 1), :])
             rows = pl.ds(r * blocks, blocks)
-            spread_ref[0, rows, cols] = top
-            spread_ref[1, rows, cols] = rest
+            spread_ref[rows, cols] = top
+            spread_ref[pl.ds((9 + r) * blocks, blocks), cols] = rest
     hot = hot_ref[...]
-    total = dot_rows(spread_ref[0], hot) + dot_rows(spread_ref[1], hot)
+    total = dot_rows(spread_ref[...], hot)
+    total = total[: 9 * blocks] + total[9 * blocks :]
     shares, _, lines, _ = share_ref.shape
     for s in range(shares):
         for r in range(9):
@@ -532,7 +531,7 @@
                 pltpu.VMEM((cells, 3, tiles, pixels), F32),
                 pltpu.VMEM((9, tiles, length), F32),
                 pltpu.VMEM((9, tiles, length), F32),
-                pltpu.VMEM((2, 9 * groups, tiles * length), jnp.bfloat16),
+                pltpu.VMEM((18 * groups, tiles * length), jnp.bfloat16),
                 pltpu.VMEM((WIDE, tiles * length), jnp.bfloat16),
                 pltpu.VMEM((groups, tiles * length), F32),
                 pltpu.VMEM((shares, 9, lines, WIDE), F32),

time: 21.3 us -> 18.9 us (0.89)
  Pallas kernels: 20.5 us -> 18.1 us
    pallas_call x1, Pallas kernels: 19.7 us -> 17.3 us  [on_device(): pl.pallas_call(functools.partial(kernel, cells, shares), name='splat_step...]
where the time goes in v3:
time: 18.9 us; the launch traced here: 18.7 us
  Pallas kernels  18.1 us (96%)
  between operations  0.64 us (3%)
    pallas_call x1, Pallas kernels, on_device(): pl.pallas_call(functools.partial(kernel, cells, shares), name='splat_step...  17.3 us
    pallas_call x1, Pallas kernels, on_device(): pl.pallas_call(finish, name='finish', out_shape=(jax.ShapeDtypeStruct(ima...  0.73 us

profile of v3, /device:TPU:11, one launch (start us, length us, event | category | flops | bytes accessed | tf_op | source)
XLA Modules:
  0.0 18.7 jit_solution(15965436868534669013)
XLA Ops:
  0.6 17.3 %splat_step.1 = (f32[3,8,256]{2,1,0:T(8,128)S(1)}, f32[59,1024]{1,0:T(8,128)S(1)}) custom-call(f32[59,4096]{1,0:T(8,128)} %gauss_in.1, s32[1,8,256]{2,1,0:T(8,128)} %lists_in.1, s32[1,8]{1,0:T(1,128)} %blocks_in.1, s32[8]{0:T(128)} %order_in.1, f32[3]{0:T(128)} %view_in.1, f32[3,8,256]{2,1,0:T(8,128)} %cot_in.1), custom_call_target="tpu_custom_call" | custom-call | tf_op jit(solution)/shard_map/splat_step/pallas_call | solution.py:499
  18.0 0.7 %finish.1 = (f32[3,8,256]{2,1,0:T(8,128)}, f32[59,1024]{1,0:T(8,128)}) custom-call(f32[3,8,256]{2,1,0:T(8,128)S(1)} %get-tuple-element.4.image_in, f32[59,1024]{1,0:T(8,128)S(1)} %get-tuple-element.5.rows_in), custom_call_target="tpu_custom_call" | custom-call | tf_op jit(solution)/shard_map/finish/pallas_call | solution.py:554

commit v4 on v3

--- a/solution.py
+++ b/solution.py
@@ -249,13 +249,15 @@
     lax.fori_loop(0, tiles, one_tile, 0, unroll=UNROLL)
 
 
-def local_backward(form_ref, glow_ref, alpha_ref, weight_ref, ends_ref):
+def local_backward(form_ref, glow_ref, alpha_ref, weight_ref, parts_ref, turned_ref, ends_ref):
     tiles, length, pixels = alpha_ref.shape
     shape = (SUBLANES, pixels)
     line = lax.broadcasted_iota(jnp.int32, shape, 0)
 
     def one_tile(t, _):
         light = dot_columns(rows_of(form_ref, t, FORM_ROWS, tiles), rows_of(glow_ref, t, FORM_ROWS, tiles))
+        for p in range(2):
+            turned_ref[t, p] = parts_ref[t, p].T
         seen = jnp.zeros(shape, F32)
         keep = jnp.ones(shape, F32)
         for v in reversed(range(length // SUBLANES)):
@@ -281,18 +283,18 @@
 
 def mark_all(index_ref, hot_ref, hit_ref):
     tiles, length = index_ref.shape
-    low_size, blocks = hot_ref.shape[0], hit_ref.shape[0]
+    low_size, blocks = hot_ref.shape[1], hit_ref.shape[0]
     for t in range(tiles):
         index = index_ref[pl.ds(t, 1), :]
         high = index // low_size
         low = index - high * low_size
         cols = pl.ds(t * length, length)
         line = lax.broadcasted_iota(jnp.int32, (low_size, length), 0)
-        hot_ref[:, cols] = jnp.where(line == low, 1.0, 0.0).astype(jnp.bfloat16)
+        hot_ref[cols, :] = jnp.where(line == low, 1.0, 0.0).astype(jnp.bfloat16).T
         hit_ref[:, cols] = jnp.where(lax.broadcasted_iota(jnp.int32, (blocks, length), 0) == high, 1.0, 0.0)
 
 
-def backward(basis_ref, alpha_ref, weight_ref, parts_ref, ends_ref, scene_ref, tint_ref, slope_ref, moments_ref):
+def backward(basis_ref, alpha_ref, weight_ref, turned_ref, ends_ref, scene_ref, tint_ref, slope_ref, moments_ref):
     tiles, length, pixels = alpha_ref.shape
     basis = basis_ref[:ROWS]
 
@@ -308,7 +310,7 @@
             slope_ref[t, 1, rows, :] = rest
         sums = dot_rows(basis, slope_ref[t, 0]) + dot_rows(basis, slope_ref[t, 1])
         tint = rows_of(tint_ref, t, ROWS, tiles)
-        colour = dot_rows(tint, parts_ref[t, 0]) + dot_rows(tint, parts_ref[t, 1])
+        colour = dot(tint, turned_ref[t, 0]) + dot(tint, turned_ref[t, 1])
         here = pl.ds(t, 1)
         for n in range(6):
             moments_ref[n, here, :] = sums[n : n + 1]
@@ -341,7 +343,7 @@
             spread_ref[rows, cols] = top
             spread_ref[pl.ds((9 + r) * blocks, blocks), cols] = rest
     hot = hot_ref[...]
-    total = dot_rows(spread_ref[...], hot)
+    total = dot(spread_ref[...], hot)
     total = total[: 9 * blocks] + total[9 * blocks :]
     shares, _, lines, _ = share_ref.shape
     for s in range(shares):
@@ -376,7 +378,7 @@
     gauss_in, lists_in, blocks_in, order_in, view_in, cot_in,
     image_ref, out_ref,
     gauss_ref, lists_ref, blocks_ref, order_ref, view_ref, cot_ref, load_sem,
-    rows_ref, table_ref, index_ref, picked_ref, form_ref, glow_ref, basis_ref, alpha_ref, weight_ref, parts_ref, slope_ref,
+    rows_ref, table_ref, index_ref, picked_ref, form_ref, glow_ref, basis_ref, alpha_ref, weight_ref, parts_ref, turned_ref, slope_ref,
     ends_ref, scene_ref, tint_ref, crit_ref, tone_ref, moments_ref, grads_ref, spread_ref, hot_ref, hit_ref,
     share_ref, came_ref, own_ref,
     crit_send, crit_recv, tone_send, tone_recv, tile_send, tile_recv,
@@ -412,7 +414,7 @@
     crit_ref[me, 1] = sum(cot_ref[ch] * tone_ref[me, ch] for ch in range(3))
     pl.semaphore_wait(barrier, cells + shares - 2)
     groups = []
-    for ref, send, recv in ((crit_ref, crit_send, crit_recv), (tone_ref, tone_send, tone_recv)):
+    def send_all(ref, send, recv):
         copies = []
         for n, peer in enumerate(cell_peers):
             copy = pltpu.make_async_remote_copy(
@@ -422,11 +424,14 @@
             )
             copy.start()
             copies.append(copy)
-        groups.append(copies)
-    local_backward(form_ref, glow_ref, alpha_ref, weight_ref, ends_ref)
+        return copies
+
+    groups.append(send_all(crit_ref, crit_send, crit_recv))
+    local_backward(form_ref, glow_ref, alpha_ref, weight_ref, parts_ref, turned_ref, ends_ref)
     mark_all(index_ref, hot_ref, hit_ref)
     for copy in groups[0]:
         copy.wait()
+    groups.append(send_all(tone_ref, tone_send, tone_recv))
 
     shape = crit_ref.shape[2:]
     light = BACKGROUND * (cot_ref[0] + cot_ref[1] + cot_ref[2])
@@ -448,7 +453,7 @@
         set_rows(tint_ref, shape[0], 3 * p, [tint[p] for tint in tints])
     set_rows(tint_ref, shape[0], 6, [jnp.zeros(shape, F32)] * (ROWS - 6))
 
-    backward(basis_ref, alpha_ref, weight_ref, parts_ref, ends_ref, scene_ref, tint_ref, slope_ref, moments_ref)
+    backward(basis_ref, alpha_ref, weight_ref, turned_ref, ends_ref, scene_ref, tint_ref, slope_ref, moments_ref)
     scatter_all(picked_ref, moments_ref, grads_ref, spread_ref, hot_ref, hit_ref, share_ref)
     copies = []
     for n, peer in enumerate(tile_peers):
@@ -523,6 +528,7 @@
                 pltpu.VMEM((tiles, length, pixels), F32),
                 pltpu.VMEM((tiles, length, pixels), F32),
                 pltpu.VMEM((tiles, 2, length, pixels), jnp.bfloat16),
+                pltpu.VMEM((tiles, 2, pixels, length), jnp.bfloat16),
                 pltpu.VMEM((tiles, 2, length, pixels), jnp.bfloat16),
                 pltpu.VMEM((tiles, 2, SUBLANES, pixels), F32),
                 pltpu.VMEM((2, tiles, pixels), F32),
@@ -532,7 +538,7 @@
                 pltpu.VMEM((9, tiles, length), F32),
                 pltpu.VMEM((9, tiles, length), F32),
                 pltpu.VMEM((18 * groups, tiles * length), jnp.bfloat16),
-                pltpu.VMEM((WIDE, tiles * length), jnp.bfloat16),
+                pltpu.VMEM((tiles * length, WIDE), jnp.bfloat16),
                 pltpu.VMEM((groups, tiles * length), F32),
                 pltpu.VMEM((shares, 9, lines, WIDE), F32),
                 pltpu.VMEM((shares - 1, 9, lines, WIDE), F32),

time: 18.9 us -> 18.2 us (0.963)
  the two profiles are of different devices: /device:TPU:11 before, /device:TPU:0 now
where the time goes in v4:
time: 18.2 us; the launch traced here: 18.1 us
  Pallas kernels  17.4 us (96%)
  between operations  0.64 us (4%)
    pallas_call x1, Pallas kernels, on_device(): pl.pallas_call(functools.partial(kernel, cells, shares), name='splat_step...  16.7 us
    pallas_call x1, Pallas kernels, on_device(): pl.pallas_call(finish, name='finish', out_shape=(jax.ShapeDtypeStruct(ima...  0.73 us

profile of v4, /device:TPU:0, one launch (start us, length us, event | category | flops | bytes accessed | tf_op | source)
XLA Modules:
  0.0 18.1 jit_solution(6809710949432910875)
XLA Ops:
  0.6 16.7 %splat_step.1 = (f32[3,8,256]{2,1,0:T(8,128)S(1)}, f32[59,1024]{1,0:T(8,128)S(1)}) custom-call(f32[59,4096]{1,0:T(8,128)} %gauss_in.1, s32[1,8,256]{2,1,0:T(8,128)} %lists_in.1, s32[1,8]{1,0:T(1,128)} %blocks_in.1, s32[8]{0:T(128)} %order_in.1, f32[3]{0:T(128)} %view_in.1, f32[3,8,256]{2,1,0:T(8,128)} %cot_in.1), custom_call_target="tpu_custom_call" | custom-call | tf_op jit(solution)/shard_map/splat_step/pallas_call | solution.py:504
  17.3 0.7 %finish.1 = (f32[3,8,256]{2,1,0:T(8,128)}, f32[59,1024]{1,0:T(8,128)}) custom-call(f32[3,8,256]{2,1,0:T(8,128)S(1)} %get-tuple-element.4.image_in, f32[59,1024]{1,0:T(8,128)S(1)} %get-tuple-element.5.rows_in), custom_call_target="tpu_custom_call" | custom-call | tf_op jit(solution)/shard_map/finish/pallas_call | solution.py:560
